TPU v7x, 32 devices: a whole 2x2x4 slice. The times are simulated.
32 devices in a mesh: grp: 4 (over y, core), leaf: 8 (over z, x).
Axes of the slice: x: 2, y: 2, z: 4, core: 2. Of those that a mesh axis runs over, the one named last changes fastest.
Arguments:
- points: bfloat16 [131072, 64], P(('grp', 'leaf')), may hold values from -6 to 6
- solution: float32 [131072, 64], P(('grp', 'leaf')), may hold values from -6 to 6
- residual: float32 [131072, 64], P(('grp', 'leaf')), may hold values from -150 to 150
- direction: float32 [131072, 64], P(('grp', 'leaf')), may hold values from -150 to 150
- near: int32 [128, 3], P(('grp', 'leaf')), may hold values from -1 to 127, as said below
- bases: bfloat16 [128, 1024, 256], P(('grp', 'leaf')), may hold values from -0.1875 to 0.1875
- leaf_transfer: bfloat16 [128, 256, 256], P(('grp', 'leaf')), may hold values from -0.1875 to 0.1875
- inner_transfer: bfloat16 [3, 2, 256, 256], replicated, may hold values from -1 to 1
- inner_coupling: bfloat16 [3, 256, 256], replicated, may hold values from -1 to 1
- outer_transfer: bfloat16 [2, 2, 256, 256], replicated, may hold values from -1 to 1
- outer_coupling: bfloat16 [2, 256, 256], replicated, may hold values from -1 to 1
Outputs:
- new_solution: float32 [131072, 64], P(('grp', 'leaf'))
- new_residual: float32 [131072, 64], P(('grp', 'leaf'))
- new_direction: float32 [131072, 64], P(('grp', 'leaf'))
Inputs may be any that keep to these rules, and one draw needn't show every extreme that they name: Row i of near is (i, i - 1 or -1, i + 1 or -1); leaf i lists i + 1 exactly when leaf i + 1 lists i; the last leaf of each aligned block of 4 leaves lists the next leaf whenever there is one.
All inputs are finite; a program needn't handle non-finite values.
Results may differ from a plain program's by a relative error of at most 0.0027.
Values may be sent and summed in bfloat16 or wider, within the bound.
A program may use at most 128 MiB of HBM per device.

v0:
```python
import jax
import jax.numpy as jnp
from jax import lax
from jax.sharding import PartitionSpec as P

highest = lax.Precision.HIGHEST
ridge = 2.0


def padded(cells, sides, width):
    for axis, dim in sides:
        count = lax.axis_size(axis)
        ends = count - 1
        head = lax.slice_in_dim(cells, 0, width, axis=dim)
        tail = lax.slice_in_dim(cells, cells.shape[dim] - width, cells.shape[dim], axis=dim)
        cells = jnp.concatenate(
            [
                lax.ppermute(tail, axis, [(i, (i + 1) % count) for i in range(ends)]),
                cells,
                lax.ppermute(head, axis, [((i + 1) % count, i) for i in range(ends)]),
            ],
            axis=dim,
        )
    return cells


def swapped(value, axis, stride):
    return lax.ppermute(value, axis, [(i, i ^ 1 << stride) for i in range(lax.axis_size(axis))])


def kernel_block(own, window, mask):
    own_wide = own.astype(jnp.float32)
    win_wide = window.astype(jnp.float32)
    sq_own = jnp.sum(own_wide * own_wide, axis=1)
    sq_win = jnp.sum(win_wide * win_wide, axis=1)
    cross = jnp.dot(own, window.T, preferred_element_type=jnp.float32)
    dist = sq_own[:, None] + sq_win[None, :] - 2.0 * cross
    return (jnp.exp(-dist * (2.0 / own.shape[1])) * mask[None, :]).astype(jnp.bfloat16)


def couple(other, side, q_level, b_level):
    left_first = side == 0
    q_mine = jnp.where(left_first, q_level[0], q_level[1])
    coupling_mat = jnp.where(left_first, b_level, b_level.T)
    return (q_mine, jnp.dot(coupling_mat, other, precision=highest))


def join_pair(own, other, side, q_level):
    left_first = side == 0
    q_mine = jnp.where(left_first, q_level[0], q_level[1])
    q_other = jnp.where(left_first, q_level[1], q_level[0])
    return jnp.dot(q_mine.T, own, precision=highest) + jnp.dot(q_other.T, other, precision=highest)


def flag_of(value):
    return jnp.where(value >= 0, 1.0, 0.0).astype(jnp.float32)


def body(
    points,
    solution,
    residual,
    direction,
    near,
    bases,
    leaf_transfer,
    inner_transfer,
    inner_coupling,
    outer_transfer,
    outer_coupling,
):
    leaf_dev = near.shape[0]
    leaf = bases.shape[1]
    dim = points.shape[1]
    nrhs = direction.shape[1]
    packed = direction.astype(jnp.bfloat16)
    joined = jnp.concatenate([points, packed], axis=1)
    extended = padded(joined, ((("grp", "leaf"), 0),), leaf)
    vectors = packed.reshape(leaf_dev, leaf, nrhs)
    skel = jnp.einsum("lpr,lpc->lrc", bases, vectors, preferred_element_type=jnp.float32)
    trans = leaf_transfer.astype(jnp.float32)
    node = jnp.einsum("lba,lbc->ac", trans, skel, precision=highest)
    inner_q = inner_transfer.astype(jnp.float32)
    inner_b = inner_coupling.astype(jnp.float32)
    outer_q = outer_transfer.astype(jnp.float32)
    outer_b = outer_coupling.astype(jnp.float32)
    records = []
    for level in range(inner_q.shape[0]):
        other = swapped(node, "leaf", level)
        side = lax.axis_index("leaf") >> level & 1
        records.append(couple(other, side, inner_q[level], inner_b[level]))
        node = join_pair(node, other, side, inner_q[level])
    for level in range(outer_q.shape[0]):
        other = swapped(node, "grp", level)
        side = lax.axis_index("grp") >> level & 1
        records.append(couple(other, side, outer_q[level], outer_b[level]))
        node = join_pair(node, other, side, outer_q[level])
    outputs = []
    for local in range(leaf_dev):
        window = extended[local * leaf : (local + 3) * leaf]
        own = points[local * leaf : (local + 1) * leaf]
        flags = near[local]
        blocks = jnp.stack([flag_of(flags[1]), jnp.ones((), jnp.float32), flag_of(flags[2])])
        mask = jnp.repeat(blocks, leaf)
        kern = kernel_block(own, window[:, :dim], mask)
        outputs.append(jnp.dot(kern, window[:, dim:], preferred_element_type=jnp.float32))
    near_term = jnp.concatenate(outputs, axis=0)
    incoming = jnp.zeros((node.shape[0], nrhs), jnp.float32)
    for q_mine, mine in reversed(records):
        incoming = mine + jnp.dot(q_mine, incoming, precision=highest)
    leaf_in = jnp.einsum("lab,bc->lac", trans, incoming, precision=highest).astype(jnp.bfloat16)
    far_term = jnp.einsum(
        "lpr,lrc->lpc", bases, leaf_in, preferred_element_type=jnp.float32
    ).reshape(-1, nrhs)
    image = ridge * direction + near_term + far_term
    rr, pq, rq, qq = lax.psum(
        (
            jnp.sum(residual * residual, axis=0),
            jnp.sum(direction * image, axis=0),
            jnp.sum(residual * image, axis=0),
            jnp.sum(image * image, axis=0),
        ),
        ("grp", "leaf"),
    )
    alpha = rr / pq
    new_solution = solution + alpha * direction
    new_residual = residual - alpha * image
    fresh = rr - 2.0 * alpha * rq + alpha * alpha * qq
    new_direction = new_residual + fresh / rr * direction
    return (new_solution, new_residual, new_direction)


def solution(mesh):
    in_specs = (
        P(("grp", "leaf"), None),
        P(("grp", "leaf"), None),
        P(("grp", "leaf"), None),
        P(("grp", "leaf"), None),
        P(("grp", "leaf"), None),
        P(("grp", "leaf"), None, None),
        P(("grp", "leaf"), None, None),
        P(),
        P(),
        P(),
        P(),
    )
    out_specs = (P(("grp", "leaf"), None), P(("grp", "leaf"), None), P(("grp", "leaf"), None))
    return jax.shard_map(body, mesh=mesh, in_specs=in_specs, out_specs=out_specs, check_vma=False)
```

profile of v0, /device:TPU:0, one launch (start us, length us, event | category | flops | bytes accessed | tf_op | source)
XLA Modules:
  0.0 146.2 jit_solution(7510675981744808651)
XLA Ops:
  0.7 1.4 convert_element_type.59
  2.1 0.4 copy-done
  2.5 0.5 fusion.17
  3.0 1.0 fusion.103
  4.0 3.0 %collective-permute-start.2 = (f32[256,64]{0,1:T(8,128)}, f32[256,64]{0,1:T(8,128)}, u32[]{:S(2)}, u32[]{:S(2)}) collective-permute-start(f32[256,64]{0,1:T(8,128)} %bitcast.13), channel_id=1, source_target_pairs={{0,1},{1,0},{2,3},{3,2},{4,5},{5,4},{6,7},{7,6},{8,9},{9,8},{10,11... | collective-permute-start | bytes 196616 | tf_op jit(solution)/shard_map/ppermute | solution.py:28
  7.0 0.8 pad_maximum_fusion.14
  7.8 2.6 %collective-permute-start = (bf16[1024,128]{0,1:T(8,128)(2,1)}, bf16[1024,128]{0,1:T(8,128)(2,1)}, u32[]{:S(2)}, u32[]{:S(2)}) collective-permute-start(bf16[1024,128]{0,1:T(8,128)(2,1)} %get-tuple-element.26), channel_id=1, source_target_pairs={{0,1},{1,2},{2,3},{3,4},{4,5},{5,6},{6,7},{7,8},{8,9},{9,10},{10,1... | collective-permute-start | bytes 786440 | tf_op jit(solution)/shard_map/ppermute | solution.py:18
  10.4 1.3 collective-permute-start.1
  11.7 0.7 multiply_reduce_fusion.11
  12.5 2.5 %convert_element_type.72 = f32[3,2,256,256]{3,2,1,0:T(8,128)} convert(bf16[3,2,256,256]{3,2,1,0:T(8,128)(2,1)} %param.18) | non-fusion elementwise | flops 393216 | bytes 2359296 | tf_op jit(solution)/shard_map/convert_element_type | solution.py:83
  14.9 2.1 %convert_element_type.74 = f32[2,2,256,256]{3,2,1,0:T(8,128)} convert(bf16[2,2,256,256]{3,2,1,0:T(8,128)(2,1)} %param.20) | non-fusion elementwise | flops 262144 | bytes 1572864 | tf_op jit(solution)/shard_map/convert_element_type | solution.py:85
  17.1 0.8 copy-done.6
  17.9 0.7 slice_bitcast_fusion.1
  18.6 1.8 %copy.18 = f32[256,256]{0,1:T(8,128)} copy(f32[256,256]{1,0:T(8,128)} %get-tuple-element.31) | data formatting | bytes 524288 | tf_op jit(solution)/shard_map/squeeze | solution.py:96
  20.4 0.8 copy.17
  21.2 1.1 convert_element_type.71
  22.3 0.9 copy-done.4
  23.2 0.9 slice_bitcast_fusion.4
  24.0 1.8 %copy.16 = f32[256,256]{0,1:T(8,128)} copy(f32[256,256]{1,0:T(8,128)} %get-tuple-element.28) | data formatting | bytes 524288 | tf_op jit(solution)/shard_map/squeeze | solution.py:91
  25.8 0.8 copy.15
  26.7 1.1 copy.14
  27.7 0.7 fusion.102
  30.9 0.6 fusion.84
  31.5 0.6 mul.157
  34.6 1.9 %fusion.50 = f32[256,64]{0,1:T(8,128)} fusion(f32[3,2,256,256]{3,2,1,0:T(8,128)} %convert_element_type.72, pred[]{:T(512)S(6)} %eq.19, f32[64,256,1]{1,0,2:T(8,128)} %fusion.103), kind=kOutput, calls=%fused_computation.92 | convolution fusion | flops 50397184 | bytes 655361 | tf_op jit(solution)/shard_map/dot_general | solution.py:52
  36.6 1.4 fusion.29
  38.0 0.6 fusion.86
  38.7 0.6 mul.179
  39.3 0.7 broadcast_in_dim.11
  40.0 0.6 mul.164
  40.6 0.7 broadcast_in_dim.12
  41.3 0.6 mul.171
  41.9 1.4 convolution_add_fusion.8
  43.3 4.5 %collective-permute-start.3 = (f32[256,64]{0,1:T(8,128)S(1)}, f32[256,64]{0,1:T(8,128)S(1)}, u32[]{:S(2)}, u32[]{:S(2)}) collective-permute-start(f32[256,64]{0,1:T(8,128)S(1)} %convolution_add_fusion.8), channel_id=1, source_target_pairs={{0,2},{1,3},{2,0},{3,1},{4,6},{5,7},{6,4},{7,5},{8,10},{9,11},{10,... | collective-permute-start | bytes 196616 | tf_op jit(solution)/shard_map/ppermute | solution.py:28
  47.8 1.3 fusion.45
  49.1 1.1 collective-permute-done.3
  50.2 1.3 convolution_add_fusion.7
  51.5 2.9 %collective-permute-start.4 = (f32[256,64]{0,1:T(8,128)S(1)}, f32[256,64]{0,1:T(8,128)S(1)}, u32[]{:S(2)}, u32[]{:S(2)}) collective-permute-start(f32[256,64]{0,1:T(8,128)S(1)} %convolution_add_fusion.7), channel_id=1, source_target_pairs={{0,4},{1,5},{2,6},{3,7},{4,0},{5,1},{6,2},{7,3},{8,12},{9,13},{10,... | collective-permute-start | bytes 196616 | tf_op jit(solution)/shard_map/ppermute | solution.py:28
  54.5 1.3 fusion.40
  55.8 1.3 collective-permute-done.4
  57.1 1.3 convolution_add_fusion.6
  58.6 0.6 fusion.35
  59.2 0.6 collective-permute-done.5
  59.8 1.2 convolution_add_fusion.1
  61.1 4.0 %collective-permute-start.6 = (f32[256,64]{1,0:T(8,128)}, f32[256,64]{1,0:T(8,128)}, u32[]{:S(2)}, u32[]{:S(2)}) collective-permute-start(f32[256,64]{1,0:T(8,128)} %convolution_add_fusion.1), channel_id=1, source_target_pairs={{0,16},{8,24},{16,0},{24,8},{1,17},{9,25},{17,1},{25,9},{2,18},{10... | collective-permute-start | bytes 196616 | tf_op jit(solution)/shard_map/ppermute | solution.py:28
  65.1 2.0 %multiply_reduce_fusion.7 = (f32[3072]{0:T(1024)}, f32[3072]{0:T(1024)}, f32[3072]{0:T(1024)}, f32[3072]{0:T(1024)S(1)}) fusion(bf16[4096,64]{0,1:T(8,128)(2,1)S(1)} %convert_element_type.59, bf16[4096,64]{0,1:T(8,128)(2,1)S(1)} %copy-done.1, bf16[1024,128]{0,1:T(8,128)(2,1)} %collective-permute-done, bf16[1024,128]{0,1:T(8,128)(2,1)} %collective-permute-done.1), kind=kLoop, calls=%fused_computation.43 | loop fusion | flops 4313088 | bytes 2408448 | tf_op jit(solution)/shard_map/reduce_sum | solution.py:35
  67.0 6.0 %fusion.10 = f32[1024,64]{0,1:T(8,128)} fusion(f32[3072]{0:T(1024)} %mul.164, f32[3072]{0:T(1024)} %get-tuple-element.13, f32[1024]{0:T(1024)} %get-tuple-element.11, bf16[4096,64]{0,1:T(8,128)(2,1)S(1)} %convert_element_type.59, bf16[4096,64]{0,1:T(8,128)(2,1)S(1)} %copy-done.1), kind=kOutput, calls=%fused_computation.14 | convolution fusion | flops 827326464 | bytes 1208320 | tf_op jit(solution)/shard_map/dot_general | solution.py:106
  73.0 6.5 %fusion.12 = f32[1024,64]{0,1:T(8,128)} fusion(f32[3072]{0:T(1024)} %mul.157, f32[3072]{0:T(1024)} %get-tuple-element.7, f32[1024]{0:T(1024)S(1)} %copy-done.24, bf16[1024,128]{0,1:T(8,128)(2,1)} %collective-permute-done, bf16[4096,64]{0,1:T(8,128)(2,1)S(1)} %convert_element_type.59, bf16[4096,64]{0,1:T(8,128)(2,1)S(1)} %copy-done.1), kind=kOutput, calls=%fused_computation.16 | convolution fusion | flops 829685760 | bytes 3043328 | tf_op jit(solution)/shard_map/dot_general | solution.py:106
  79.6 6.4 %fusion.13 = f32[1024,64]{0,1:T(8,128)} fusion(f32[3072]{0:T(1024)} %mul.179, f32[3072]{0:T(1024)} %get-tuple-element.8, f32[1024]{0:T(1024)} %get-tuple-element.12, bf16[1024,128]{0,1:T(8,128)(2,1)} %collective-permute-done.1, bf16[4096,64]{0,1:T(8,128)(2,1)S(1)} %convert_element_type.59, bf16[4096,64]{0,1:T(8,128)(2,1)S(1)} %copy-done.1), kind=kOutput, calls=%fused_computation.17 | convolution fusion | flops 829685760 | bytes 3043328 | tf_op jit(solution)/shard_map/dot_general | solution.py:106
  86.0 6.0 %fusion.11 = f32[1024,64]{0,1:T(8,128)} fusion(f32[3072]{0:T(1024)} %mul.171, f32[3072]{0:T(1024)S(1)} %get-tuple-element.14, f32[1024]{0:T(1024)S(1)} %copy-done.23, bf16[4096,64]{0,1:T(8,128)(2,1)S(1)} %convert_element_type.59, bf16[4096,64]{0,1:T(8,128)(2,1)S(1)} %copy-done.1), kind=kOutput, calls=%fused_computation.15 | convolution fusion | flops 827326464 | bytes 1208320 | tf_op jit(solution)/shard_map/dot_general | solution.py:106
  92.0 1.6 %convolution_add_fusion = f32[256,64]{1,0:T(8,128)S(1)} fusion(f32[256,64]{1,0:T(8,128)S(1)} %fusion.29, f32[256,64]{1,0:T(8,128)} %collective-permute-done.6, f32[256,256]{0,1:T(8,128)} %copy.18, pred[]{:T(512)S(6)} %eq.23, f32[2,256,256]{2,1,0:T(8,128)} %copy-done.6), kind=kOutput, calls=%fused_computation.21 | convolution fusion | flops 50413568 | bytes 786433 | tf_op jit(solution)/shard_map/dot_general | solution.py:45
  93.6 1.4 fusion.33
  95.1 1.4 convolution_add_fusion.2
  96.5 0.4 fusion.38
  96.9 1.3 convolution_add_fusion.3
  98.2 0.4 fusion.43
  98.6 0.6 convolution_add_fusion.4
  99.2 0.4 fusion.48
  99.6 1.2 fusion.15
  100.8 0.6 fusion.14
  101.5 0.7 convolution_bitcast_fusion
  103.3 1.5 %multiply_reduce_fusion.1 = (f32[64]{0:T(128)S(1)}, f32[64]{0:T(128)S(1)}, f32[64]{0:T(128)S(1)}, f32[64]{0:T(128)S(1)}, f32[4096,64]{0,1:T(8,128)}) fusion(f32[4096,64]{0,1:T(8,128)S(1)} %copy-done.8, f32[4096,64]{0,1:T(8,128)S(1)} %copy-done.3, f32[4096,64]{0,1:T(8,128)S(1)} %bitcast.152, f32[1024,64]{0,1:T(8,128)S(1)} %copy-done.15, ...), kind=kLoop, calls=%fused_computation.35 | loop fusion | flops 3669760 | bytes 5243904 | tf_op jit(solution)/shard_map/reduce_sum | solution.py:120
  104.8 37.6 %all-reduce = (f32[64]{0:T(128)S(1)}, f32[64]{0:T(128)S(1)}, f32[64]{0:T(128)S(1)}, f32[64]{0:T(128)S(1)}) all-reduce(f32[64]{0:T(128)S(1)} %get-tuple-element.6, f32[64]{0:T(128)S(1)} %get-tuple-element.5, f32[64]{0:T(128)S(1)} %get-tuple-element.4, f32[64]{0:T(128)S(1)} %get-tuple-element.3), channel_id=1, replica_groups=mesh['grp'=4,'leaf'=8] {'grp','leaf'}, use_global_device_ids=true, to_apply=%region_1.2 | all-reduce | flops 256 | bytes 2048 | tf_op jit(solution)/shard_map/psum | solution.py:116
  142.4 3.8 %multiply_add_fusion = (f32[4096,64]{0,1:T(8,128)}, f32[4096,64]{0,1:T(8,128)}, f32[4096,64]{0,1:T(8,128)}) fusion(f32[4096,64]{0,1:T(8,128)S(1)} %copy-done.3, f32[64]{0:T(128)S(1)} %get-tuple-element.21, f32[4096,64]{0,1:T(8,128)} %param.13, f32[4096,64]{0,1:T(8,128)} %get-tuple-element.23, f32[64]{0:T(128)S(1)} %get-tuple-element.22, f32[4096,64]{0,1:T(8,128)} %param.12), kind=kLoop, calls=%fused_computation.33 | loop fusion | flops 1572864 | bytes 7340544 | tf_op jit(solution)/shard_map/add | solution.py:129
  (57 shorter events, 1.4 us)
Async XLA Ops:
  0.6 1.9 %copy-start = (bf16[4,1024,256]{2,1,0:T(8,128)(2,1)S(1)}, bf16[4,1024,256]{2,1,0:T(8,128)(2,1)}, u32[]{:S(2)}) copy-start(bf16[4,1024,256]{2,1,0:T(8,128)(2,1)} %param.16) | copy-start | bytes 6291460
  0.6 2.4 %copy-start.9 = (bf16[4,256,256]{2,1,0:T(8,128)(2,1)S(1)}, bf16[4,256,256]{2,1,0:T(8,128)(2,1)}, u32[]{:S(2)}) copy-start(bf16[4,256,256]{2,1,0:T(8,128)(2,1)} %param.17) | copy-start | bytes 1572868
  2.1 4.9 %copy-start.1 = (bf16[4096,64]{0,1:T(8,128)(2,1)S(1)}, bf16[4096,64]{0,1:T(8,128)(2,1)}, u32[]{:S(2)}) copy-start(bf16[4096,64]{0,1:T(8,128)(2,1)} %param.11) | copy-start | bytes 1572868
  4.0 37.9 %collective-permute-start.2 = (f32[256,64]{0,1:T(8,128)}, f32[256,64]{0,1:T(8,128)}, u32[]{:S(2)}, u32[]{:S(2)}) collective-permute-start(f32[256,64]{0,1:T(8,128)} %bitcast.13), channel_id=1, source_target_pairs={{0,1},{1,0},{2,3},{3,2},{4,5},{5,4},{6,7},{7,6},{8,9},{9,8},{10,11... | collective-permute-start | bytes 196616 | tf_op jit(solution)/shard_map/ppermute | solution.py:28
  7.8 57.3 %collective-permute-start = (bf16[1024,128]{0,1:T(8,128)(2,1)}, bf16[1024,128]{0,1:T(8,128)(2,1)}, u32[]{:S(2)}, u32[]{:S(2)}) collective-permute-start(bf16[1024,128]{0,1:T(8,128)(2,1)} %get-tuple-element.26), channel_id=1, source_target_pairs={{0,1},{1,2},{2,3},{3,4},{4,5},{5,6},{6,7},{7,8},{8,9},{9,10},{10,1... | collective-permute-start | bytes 786440 | tf_op jit(solution)/shard_map/ppermute | solution.py:18
  10.4 54.6 %collective-permute-start.1 = (bf16[1024,128]{0,1:T(8,128)(2,1)}, bf16[1024,128]{0,1:T(8,128)(2,1)}, u32[]{:S(2)}, u32[]{:S(2)}) collective-permute-start(bf16[1024,128]{0,1:T(8,128)(2,1)} %get-tuple-element.25), channel_id=1, source_target_pairs={{1,0},{2,1},{3,2},{4,3},{5,4},{6,5},{7,6},{8,7},{9,8},{10,9},{11,1... | collective-permute-start | bytes 786440 | tf_op jit(solution)/shard_map/ppermute | solution.py:20
  12.5 4.6 %copy-start.12 = (bf16[2,256,256]{2,1,0:T(8,128)(2,1)S(1)}, bf16[2,256,256]{2,1,0:T(8,128)(2,1)}, u32[]{:S(2)}) copy-start(bf16[2,256,256]{2,1,0:T(8,128)(2,1)} %param.21) | copy-start | bytes 786436
  17.1 0.8 copy-start.6
  21.2 6.5 %copy-start.22 = (s32[4,3]{1,0:T(4,128)S(1)}, s32[4,3]{1,0:T(4,128)}, u32[]{:S(2)}) copy-start(s32[4,3]{1,0:T(4,128)} %param.15) | copy-start | bytes 148
  22.3 0.9 copy-start.4
  41.9 16.7 %copy-start.7 = (f32[2,2,256,256]{3,2,1,0:T(8,128)S(1)}, f32[2,2,256,256]{3,2,1,0:T(8,128)}, u32[]{:S(2)}) copy-start(f32[2,2,256,256]{3,2,1,0:T(8,128)} %convert_element_type.74) | copy-start | bytes 3145732
  43.3 6.9 %collective-permute-start.3 = (f32[256,64]{0,1:T(8,128)S(1)}, f32[256,64]{0,1:T(8,128)S(1)}, u32[]{:S(2)}, u32[]{:S(2)}) collective-permute-start(f32[256,64]{0,1:T(8,128)S(1)} %convolution_add_fusion.8), channel_id=1, source_target_pairs={{0,2},{1,3},{2,0},{3,1},{4,6},{5,7},{6,4},{7,5},{8,10},{9,11},{10,... | collective-permute-start | bytes 196616 | tf_op jit(solution)/shard_map/ppermute | solution.py:28
  50.2 8.3 %copy-start.17 = (f32[256,64]{0,1:T(8,128)}, f32[256,64]{0,1:T(8,128)S(1)}, u32[]{:S(2)}) copy-start(f32[256,64]{0,1:T(8,128)S(1)} %collective-permute-done.3) | copy-start | bytes 196612
  51.5 5.6 %collective-permute-start.4 = (f32[256,64]{0,1:T(8,128)S(1)}, f32[256,64]{0,1:T(8,128)S(1)}, u32[]{:S(2)}, u32[]{:S(2)}) collective-permute-start(f32[256,64]{0,1:T(8,128)S(1)} %convolution_add_fusion.7), channel_id=1, source_target_pairs={{0,4},{1,5},{2,6},{3,7},{4,0},{5,1},{6,2},{7,3},{8,12},{9,13},{10,... | collective-permute-start | bytes 196616 | tf_op jit(solution)/shard_map/ppermute | solution.py:28
  57.1 1.4 copy-start.19
  58.5 1.3 collective-permute-start.5
  59.8 1.2 copy-start.21
  61.1 31.0 %collective-permute-start.6 = (f32[256,64]{1,0:T(8,128)}, f32[256,64]{1,0:T(8,128)}, u32[]{:S(2)}, u32[]{:S(2)}) collective-permute-start(f32[256,64]{1,0:T(8,128)} %convolution_add_fusion.1), channel_id=1, source_target_pairs={{0,16},{8,24},{16,0},{24,8},{1,17},{9,25},{17,1},{25,9},{2,18},{10... | collective-permute-start | bytes 196616 | tf_op jit(solution)/shard_map/ppermute | solution.py:28
  67.0 6.0 %copy-start.24 = (f32[1024]{0:T(1024)S(1)}, f32[1024]{0:T(1024)}, u32[]{:S(2)}) copy-start(f32[1024]{0:T(1024)} %get-tuple-element.9) | copy-start | bytes 12292
  79.6 6.4 %copy-start.23 = (f32[1024]{0:T(1024)S(1)}, f32[1024]{0:T(1024)}, u32[]{:S(2)}) copy-start(f32[1024]{0:T(1024)} %get-tuple-element.10) | copy-start | bytes 12292
  92.0 4.4 %copy-start.2 = (f32[3,2,256,256]{3,2,1,0:T(8,128)S(1)}, f32[3,2,256,256]{3,2,1,0:T(8,128)}, u32[]{:S(2)}) copy-start(f32[3,2,256,256]{3,2,1,0:T(8,128)} %convert_element_type.72) | copy-start | bytes 4718596
  92.0 4.9 %copy-start.5 = (f32[3,256,256]{2,1,0:T(8,128)S(1)}, f32[3,256,256]{2,1,0:T(8,128)}, u32[]{:S(2)}) copy-start(f32[3,256,256]{2,1,0:T(8,128)} %copy-done.4) | copy-start | bytes 2359300
  92.0 4.9 %copy-start.20 = (f32[256,64]{0,1:T(8,128)S(1)}, f32[256,64]{0,1:T(8,128)}, u32[]{:S(2)}) copy-start(f32[256,64]{0,1:T(8,128)} %copy-done.19) | copy-start | bytes 196612
  92.0 6.6 %copy-start.11 = (f32[256,256]{0,1:T(8,128)S(1)}, f32[256,256]{0,1:T(8,128)}, u32[]{:S(2)}) copy-start(f32[256,256]{0,1:T(8,128)} %copy.15) | copy-start | bytes 786436
  92.0 6.6 %copy-start.18 = (f32[256,64]{0,1:T(8,128)S(1)}, f32[256,64]{0,1:T(8,128)}, u32[]{:S(2)}) copy-start(f32[256,64]{0,1:T(8,128)} %copy-done.17) | copy-start | bytes 196612
  96.5 4.3 %copy-start.10 = (bf16[4,256,256]{2,1,0:T(8,128)(2,1)S(1)}, bf16[4,256,256]{2,1,0:T(8,128)(2,1)}, u32[]{:S(2)}) copy-start(bf16[4,256,256]{2,1,0:T(8,128)(2,1)} %param.17) | copy-start | bytes 1572868
  101.5 1.2 copy-start.3
  101.5 1.5 %copy-start.8 = (f32[4096,64]{0,1:T(8,128)S(1)}, f32[4096,64]{0,1:T(8,128)}, u32[]{:S(2)}) copy-start(f32[4096,64]{0,1:T(8,128)} %param.13) | copy-start | bytes 3145732
  101.5 1.6 %copy-start.13 = (f32[1024,64]{0,1:T(8,128)S(1)}, f32[1024,64]{0,1:T(8,128)}, u32[]{:S(2)}) copy-start(f32[1024,64]{0,1:T(8,128)} %fusion.10) | copy-start | bytes 786436
  101.5 1.6 %copy-start.14 = (f32[1024,64]{0,1:T(8,128)S(1)}, f32[1024,64]{0,1:T(8,128)}, u32[]{:S(2)}) copy-start(f32[1024,64]{0,1:T(8,128)} %fusion.12) | copy-start | bytes 786436
  101.5 1.7 %copy-start.15 = (f32[1024,64]{0,1:T(8,128)S(1)}, f32[1024,64]{0,1:T(8,128)}, u32[]{:S(2)}) copy-start(f32[1024,64]{0,1:T(8,128)} %fusion.13) | copy-start | bytes 786436
  101.5 1.8 %copy-start.16 = (f32[1024,64]{0,1:T(8,128)S(1)}, f32[1024,64]{0,1:T(8,128)}, u32[]{:S(2)}) copy-start(f32[1024,64]{0,1:T(8,128)} %fusion.11) | copy-start | bytes 786436
where the time goes:
time: 147 us; the launch traced here: 146 us
  matrix products  48.3 us (33%)
  blocking collectives  37.6 us (26%)
  starting transfers between devices  18.4 us (13%)
  other arithmetic  17.2 us (12%)
  local copies, waits for them, and re-layouts  15.7 us (11%)
  between operations  5.92 us (4%)
  waiting for transfers between devices  3.06 us (2%)
    psum x1, blocking collectives, body(): lax.psum((jnp.sum(residual * residual, axis=0), jnp.sum(direction * image...  37.6 us
    dot_general x4, matrix products, body(): jnp.dot(kern, window[:, dim:], preferred_element_type=jnp.float32)  25 us
    ppermute x5, starting transfers between devices, swapped(): lax.ppermute(value, axis, [(i, i ^ 1 << stride) for i in range(lax.axis_s...  14.5 us
    dot_general x5, matrix products, couple(): return (q_mine, jnp.dot(coupling_mat, other, precision=highest))  6.09 us
    dot_general x4, matrix products, join_pair(): jnp.dot(q_other.T, other, precision=highest)  5.34 us
    dot_general x4, matrix products, join_pair(): jnp.dot(q_mine.T, own, precision=highest)  5.18 us
    squeeze x4, local copies, waits for them, and re-layouts, body(): records.append(couple(other, side, inner_q[level], inner_b[level]))  4.55 us
    dot_general x5, matrix products, body(): incoming = mine + jnp.dot(q_mine, incoming, precision=highest)  3.93 us
  transfers between devices with their start and end apart: 7, of which 3 were waited for; matrix products, arithmetic and copies ran while one was open for 41% of the time, Pallas kernels for 0%

commit v1 on v0

v1 whole, which is shorter than its diff:
```python
import functools
import math

import jax
import jax.numpy as jnp
from jax import lax
from jax.experimental import pallas as pl
from jax.experimental.pallas import tpu as pltpu
from jax.sharding import PartitionSpec as P

MESH = pl.DeviceIdType.MESH
ridge = 2.0
f32 = jnp.float32
bf16 = jnp.bfloat16
vmem = pl.BlockSpec(memory_space=pltpu.VMEM)
smem = pl.BlockSpec(memory_space=pltpu.SMEM)


def nn(a, b):
    return jnp.dot(a, b, preferred_element_type=f32)


def nt(a, b):
    return lax.dot_general(a, b, (((1,), (1,)), ((), ())), preferred_element_type=f32)


def split(value):
    high = value.astype(bf16)
    low = (value - high.astype(f32)).astype(bf16)
    return jnp.concatenate([high, low], axis=0)


def fold(stacked):
    half = stacked.shape[0] // 2
    return stacked[:half] + stacked[half:]


def upward_kernel(points_ref, direction_ref, bases_ref, trans_ref, joint_ref, node_ref, acc):
    step = pl.program_id(0)
    dim = points_ref.shape[0]
    packed = direction_ref[...].astype(bf16)
    joint_ref[:dim, :] = points_ref[...]
    joint_ref[dim:, :] = packed
    term = fold(nn(split(nn(packed, bases_ref[0])), trans_ref[0]))

    @pl.when(step == 0)
    def _():
        acc[...] = term

    @pl.when(step > 0)
    def _():
        acc[...] += term

    @pl.when(step == pl.num_programs(0) - 1)
    def _():
        node_ref[...] = split(acc[...])


def tree_kernel(
    groups, leaves, leaf, node_ref, joint_ref, inner_q, inner_b, outer_q, outer_b,
    incoming_ref, halo_ref, sent, got, node_send, node_recv, halo_send, halo_recv,
):
    grp = lax.axis_index("grp")
    pos = lax.axis_index("leaf")
    inner = inner_q.shape[0]
    outer = outer_q.shape[0]
    me = grp * leaves + pos
    count = groups * leaves
    right = lax.rem(me + 1, count)
    left = lax.rem(me + count - 1, count)
    right_id = (right // leaves, lax.rem(right, leaves))
    left_id = (left // leaves, lax.rem(left, leaves))
    levels = []
    for k in range(inner):
        bit = lax.rem(pos // (1 << k), 2)
        levels.append((bit, (grp, pos + (1 - 2 * bit) * (1 << k)), inner_q, inner_b, k))
    for k in range(outer):
        bit = lax.rem(grp // (1 << k), 2)
        levels.append((bit, (grp + (1 - 2 * bit) * (1 << k), pos), outer_q, outer_b, k))

    barrier = pltpu.get_barrier_semaphore()
    for who in [left_id, right_id] + [lv[1] for lv in levels]:
        pl.semaphore_signal(barrier, inc=1, device_id=who, device_id_type=MESH)
    pl.semaphore_wait(barrier, 2 + len(levels))

    last = joint_ref.shape[1] - leaf
    halos = [
        pltpu.make_async_remote_copy(
            src_ref=joint_ref.at[:, pl.ds(last, leaf)], dst_ref=halo_ref.at[0],
            send_sem=halo_send.at[0], recv_sem=halo_recv.at[0], device_id=right_id, device_id_type=MESH,
        ),
        pltpu.make_async_remote_copy(
            src_ref=joint_ref.at[:, pl.ds(0, leaf)], dst_ref=halo_ref.at[1],
            send_sem=halo_send.at[1], recv_sem=halo_recv.at[1], device_id=left_id, device_id_type=MESH,
        ),
    ]

    def coupled(n):
        bit, _, _, b_ref, k = levels[n]
        other = got[n]
        mat = b_ref[k]
        return fold(jnp.where(bit == 0, nt(other, mat), nn(other, mat)))

    records = []
    for n, (bit, partner, q_ref, b_ref, k) in enumerate(levels):
        source = node_ref if n == 0 else sent.at[n]
        copy = pltpu.make_async_remote_copy(
            src_ref=source, dst_ref=got.at[n], send_sem=node_send.at[n], recv_sem=node_recv.at[n],
            device_id=partner, device_id_type=MESH,
        )
        copy.start()
        if n == 0:
            for halo in halos:
                halo.start()
        else:
            records.append(coupled(n - 1))
        final = n == len(levels) - 1
        if not final:
            mine = nn(source[...], q_ref[k, bit])
        copy.wait()
        if not final:
            sent[n + 1] = split(fold(mine + nn(got[n], q_ref[k, 1 - bit])))
    incoming = coupled(len(levels) - 1)
    for n in reversed(range(len(levels) - 1)):
        bit, _, q_ref, _, k = levels[n]
        incoming = records[n] + fold(nt(split(incoming), q_ref[k, bit]))
    incoming_ref[...] = incoming
    for halo in halos:
        halo.wait()


def near_kernel(near_ref, joint_ref, halo_ref, out_ref, source, target):
    leaf_dev = near_ref.shape[0]
    rows = joint_ref.shape[0]
    leaf = halo_ref.shape[2]
    nrhs = out_ref.shape[0]
    dim = rows - nrhs
    tile = min(leaf, 256)
    scale = 2.0 / dim * math.log2(math.e)

    def parts(pts):
        wide = pts.astype(f32)
        sq = jnp.sum(wide * wide, axis=0, keepdims=True)
        high = sq.astype(bf16).astype(f32)
        mid = (sq - high).astype(bf16).astype(f32)
        low = sq - high - mid
        row = lax.broadcasted_iota(jnp.int32, (128 - dim, pts.shape[1]), 0)

        def extra(first, second):
            ones = jnp.where(jnp.logical_and(row >= second, row < second + 3), 1.0, 0.0)
            return jnp.where(row == first, -high, jnp.where(row == first + 1, -mid, jnp.where(row == first + 2, -low, ones)))

        return wide, extra

    def put_source(slot, pts):
        wide, extra = parts(pts)
        source[slot] = jnp.concatenate([2.0 * wide, extra(0, 3)], axis=0).T.astype(bf16)

    put_source(0, halo_ref[0, :dim, :])
    put_source(leaf_dev + 1, halo_ref[1, :dim, :])

    @pl.loop(0, leaf_dev)
    def _(i):
        pts = joint_ref[:dim, pl.ds(pl.multiple_of(i * leaf, leaf), leaf)]
        put_source(i + 1, pts)
        wide, extra = parts(pts)
        target[i] = jnp.concatenate([wide, extra(3, 0)], axis=0).astype(bf16)

    def block(i, slot, values):
        acc = jnp.zeros((nrhs, leaf), f32)
        for t in range(leaf // tile):
            power = nn(source[slot, t * tile : (t + 1) * tile, :], target[i])
            kern = jnp.exp2(power * scale).astype(bf16)
            acc += nn(values(t), kern)
        return acc

    def own(j):
        def values(t):
            return joint_ref[dim:, pl.ds(pl.multiple_of(j * leaf + t * tile, tile), tile)]

        return values

    def edge(side):
        return lambda t: halo_ref[side, dim:, t * tile : (t + 1) * tile]

    def flag(i, column):
        return jnp.where(near_ref[i, column] >= 0, 1.0, 0.0).astype(f32)

    @pl.loop(0, leaf_dev)
    def _(i):
        out_ref[:, pl.ds(pl.multiple_of(i * leaf, leaf), leaf)] = block(i, i + 1, own(i))

    @pl.loop(0, leaf_dev - 1)
    def _(i):
        here = pl.ds(pl.multiple_of(i * leaf, leaf), leaf)
        out_ref[:, here] += flag(i, 2) * block(i, i + 2, own(i + 1))
        there = pl.ds(pl.multiple_of(i * leaf + leaf, leaf), leaf)
        out_ref[:, there] += flag(i + 1, 1) * block(i + 1, i + 1, own(i))

    out_ref[:, :leaf] += flag(0, 1) * block(0, 0, edge(0))
    out_ref[:, (leaf_dev - 1) * leaf :] += flag(leaf_dev - 1, 2) * block(leaf_dev - 1, leaf_dev + 1, edge(1))


def total_kernel(
    groups, leaves, incoming_ref, trans_ref, bases_ref, near_ref, direction_ref, residual_ref,
    image_ref, sums_ref, first, second, first_send, first_recv, second_send, second_recv,
):
    grp = lax.axis_index("grp")
    pos = lax.axis_index("leaf")
    barrier = pltpu.get_barrier_semaphore()
    for o in range(1, leaves):
        pl.semaphore_signal(barrier, inc=1, device_id=(grp, lax.rem(pos + o, leaves)), device_id_type=MESH)
    for o in range(1, groups):
        pl.semaphore_signal(barrier, inc=1, device_id=(lax.rem(grp + o, groups), pos), device_id_type=MESH)

    leaf_dev, leaf = bases_ref.shape[:2]
    nrhs = direction_ref.shape[0]
    stacked = split(incoming_ref[...])
    sums = [jnp.zeros((nrhs, 128), f32)] * 4

    def narrow(value):
        out = value[:, :128]
        for c in range(1, value.shape[1] // 128):
            out += value[:, c * 128 : (c + 1) * 128]
        return out

    for i in range(leaf_dev):
        cols = slice(i * leaf, (i + 1) * leaf)
        leaf_in = fold(nt(stacked, trans_ref[i])).astype(bf16)
        way = direction_ref[:, cols]
        rest = residual_ref[:, cols]
        image = ridge * way + near_ref[:, cols] + nt(leaf_in, bases_ref[i])
        image_ref[:, cols] = image
        terms = (rest * rest, way * image, rest * image, image * image)
        sums = [s + narrow(t) for s, t in zip(sums, terms)]
    rows = [jnp.sum(s.T, axis=0, keepdims=True) for s in sums]
    first[pos] = jnp.concatenate(rows + [jnp.zeros((4, nrhs), f32)], axis=0)
    pl.semaphore_wait(barrier, leaves - 1 + groups - 1)

    def exchange(slots, mine, count, send, recv, where):
        def copy(o, slot):
            return pltpu.make_async_remote_copy(
                src_ref=slots.at[slot], dst_ref=slots.at[slot], send_sem=send.at[o], recv_sem=recv.at[slot],
                device_id=where(lax.rem(mine + o, count)), device_id_type=MESH,
            )

        for o in range(1, count):
            copy(o, mine).start()
        for o in range(1, count):
            copy(o, lax.rem(mine + o, count)).wait_recv()
        for o in range(1, count):
            copy(o, mine).wait_send()
        out = slots[0]
        for s in range(1, count):
            out += slots[s]
        return out

    second[grp] = exchange(first, pos, leaves, first_send, first_recv, lambda t: (grp, t))
    sums_ref[...] = exchange(second, grp, groups, second_send, second_recv, lambda t: (t, pos))


def body(groups, leaves, points, solution, residual, direction, near, bases, leaf_transfer,
         inner_transfer, inner_coupling, outer_transfer, outer_coupling):
    leaf_dev = near.shape[0]
    leaf, rank = bases.shape[1:]
    count, dim = points.shape
    nrhs = direction.shape[1]
    rows = dim + nrhs
    levels = inner_transfer.shape[0] + outer_transfer.shape[0]
    p, x, r, d = points.T, solution.T, residual.T, direction.T
    joint, node = pl.pallas_call(
        upward_kernel,
        grid=(leaf_dev,),
        in_specs=[
            pl.BlockSpec((dim, leaf), lambda i: (0, i)),
            pl.BlockSpec((nrhs, leaf), lambda i: (0, i)),
            pl.BlockSpec((1, leaf, rank), lambda i: (i, 0, 0)),
            pl.BlockSpec((1, rank, rank), lambda i: (i, 0, 0)),
        ],
        out_specs=[
            pl.BlockSpec((rows, leaf), lambda i: (0, i)),
            pl.BlockSpec((2 * nrhs, rank), lambda i: (0, 0)),
        ],
        out_shape=[
            jax.ShapeDtypeStruct((rows, count), bf16),
            jax.ShapeDtypeStruct((2 * nrhs, rank), bf16),
        ],
        scratch_shapes=[pltpu.VMEM((nrhs, rank), f32)],
        name="upward",
    )(p, d, bases, leaf_transfer)
    incoming, halo = pl.pallas_call(
        functools.partial(tree_kernel, groups, leaves, leaf),
        in_specs=[vmem] * 6,
        out_specs=[vmem] * 2,
        out_shape=[
            jax.ShapeDtypeStruct((nrhs, rank), f32),
            jax.ShapeDtypeStruct((2, rows, leaf), bf16),
        ],
        scratch_shapes=[
            pltpu.VMEM((levels, 2 * nrhs, rank), bf16),
            pltpu.VMEM((levels, 2 * nrhs, rank), bf16),
            pltpu.SemaphoreType.DMA((levels,)),
            pltpu.SemaphoreType.DMA((levels,)),
            pltpu.SemaphoreType.DMA((2,)),
            pltpu.SemaphoreType.DMA((2,)),
        ],
        compiler_params=pltpu.CompilerParams(collective_id=0, has_side_effects=True),
        name="tree",
    )(node, joint, inner_transfer, inner_coupling, outer_transfer, outer_coupling)
    near_term = pl.pallas_call(
        near_kernel,
        in_specs=[smem, vmem, vmem],
        out_specs=vmem,
        out_shape=jax.ShapeDtypeStruct((nrhs, count), f32),
        scratch_shapes=[
            pltpu.VMEM((leaf_dev + 2, leaf, 128), bf16),
            pltpu.VMEM((leaf_dev, 128, leaf), bf16),
        ],
        name="near",
    )(near, joint, halo)
    image, sums = pl.pallas_call(
        functools.partial(total_kernel, groups, leaves),
        in_specs=[vmem] * 6,
        out_specs=[vmem] * 2,
        out_shape=[
            jax.ShapeDtypeStruct((nrhs, count), f32),
            jax.ShapeDtypeStruct((8, nrhs), f32),
        ],
        scratch_shapes=[
            pltpu.VMEM((leaves, 8, nrhs), f32),
            pltpu.VMEM((groups, 8, nrhs), f32),
            pltpu.SemaphoreType.DMA((leaves,)),
            pltpu.SemaphoreType.DMA((leaves,)),
            pltpu.SemaphoreType.DMA((groups,)),
            pltpu.SemaphoreType.DMA((groups,)),
        ],
        compiler_params=pltpu.CompilerParams(collective_id=1, has_side_effects=True),
        name="total",
    )(incoming, leaf_transfer, bases, near_term, d, r)
    rr, pq, rq, qq = sums[0], sums[1], sums[2], sums[3]
    alpha = rr / pq
    fresh = rr - 2.0 * alpha * rq + alpha * alpha * qq
    beta = fresh / rr
    new_residual = r - alpha[:, None] * image
    return (
        (x + alpha[:, None] * d).T,
        new_residual.T,
        (new_residual + beta[:, None] * d).T,
    )


def solution(mesh):
    both = ("grp", "leaf")
    flat = P(both, None)
    deep = P(both, None, None)
    return jax.shard_map(
        functools.partial(body, mesh.shape["grp"], mesh.shape["leaf"]),
        mesh=mesh,
        in_specs=(flat, flat, flat, flat, flat, deep, deep, P(), P(), P(), P()),
        out_specs=(flat, flat, flat),
        check_vma=False,
    )
```

time: 147 us -> 71.1 us (0.48)
  Pallas kernels: 0 us -> 65.2 us
  matrix products: 48.3 us -> 0 us
  blocking collectives: 37.6 us -> 0 us
  starting transfers between devices: 18.4 us -> 0 us
  local copies, waits for them, and re-layouts: 15.7 us -> 0.01 us
  other arithmetic: 17.2 us -> 4.89 us
  between operations: 5.92 us -> 0.66 us
  waiting for transfers between devices: 3.06 us -> 0 us
    pallas_call x0 -> x4, Pallas kernels: none -> 65.2 us  [the longest x1 30 us: body(): pl.pallas_call(functools.partial(tree_kernel, groups, leaves, leaf), in_s...]
    dot_general x26 -> x0, matrix products: 48.3 us -> none  [the longest x4 25 us: body(): jnp.dot(kern, window[:, dim:], preferred_element_type=jnp.float32)]
    psum x1 -> x0, blocking collectives: 37.6 us -> none  [body(): lax.psum((jnp.sum(residual * residual, axis=0), jnp.sum(direction * image...]
    ppermute x7 -> x0, starting transfers between devices: 18.4 us -> none  [the longest x5 14.5 us: swapped(): lax.ppermute(value, axis, [(i, i ^ 1 << stride) for i in range(lax.axis_s...]
    squeeze x7 -> x0, local copies, waits for them, and re-layouts: 7.9 us -> none  [the longest x4 4.55 us: body(): records.append(couple(other, side, inner_q[level], inner_b[level]))]
    convert_element_type x5 -> x0, other arithmetic: 7.11 us -> none  [the longest x1 2.48 us: body(): inner_q = inner_transfer.astype(jnp.float32)]
    reduce_sum x3 -> x0, other arithmetic: 4.2 us -> none  [the longest x1 1.97 us: kernel_block(): sq_win = jnp.sum(win_wide * win_wide, axis=1)]
    unnamed x50 -> x6, local copies, waits for them, and re-layouts: 3.12 us -> 0.01 us
  transfers between devices with their start and end apart: 7 -> 0, of which waited for: 3 -> 0; matrix products, arithmetic and copies ran while one was open for 41% -> 0% of each run, Pallas kernels for 0% -> 0%
where the time goes in v1:
time: 71.1 us; the launch traced here: 70.8 us
  Pallas kernels  65.2 us (92%)
  other arithmetic  4.89 us (7%)
    pallas_call x1, Pallas kernels, body(): pl.pallas_call(functools.partial(tree_kernel, groups, leaves, leaf), in_s...  30 us
    pallas_call x1, Pallas kernels, body(): pl.pallas_call(near_kernel, in_specs=[smem, vmem, vmem], out_specs=vmem,...  18 us
    pallas_call x1, Pallas kernels, body(): pl.pallas_call(functools.partial(total_kernel, groups, leaves), in_specs=...  12.5 us
    pallas_call x1, Pallas kernels, body(): pl.pallas_call(upward_kernel, grid=(leaf_dev,), in_specs=[pl.BlockSpec((d...  4.7 us
    transpose x1, other arithmetic, body(): return ((x + alpha[:, None] * d).T, new_residual.T, (new_residual + beta[...  2.88 us

profile of v1, /device:TPU:0, one launch (start us, length us, event | category | flops | bytes accessed | tf_op | source)
XLA Modules:
  0.0 70.8 jit_solution(13512977411419859471)
XLA Ops:
  0.6 4.7 %upward.1 = (bf16[128,4096]{1,0:T(8,128)(2,1)}, bf16[128,256]{1,0:T(8,128)(2,1)}) custom-call(bf16[64,4096]{1,0:T(8,128)(2,1)} %bitcast.32, f32[64,4096]{1,0:T(8,128)} %bitcast.29, bf16[4,1024,256]{2,1,0:T(8,128)(2,1)} %bases_ref.3, bf16[4,256,256]{2,1,0:T(8,128)(2,1)} %trans_ref.3), custom_call_target="tpu_custom_call" | custom-call | tf_op jit(solution)/shard_map/upward/pallas_call | solution.py:271
  5.3 30.0 %tree.1 = (f32[64,256]{1,0:T(8,128)}, bf16[2,128,1024]{2,1,0:T(8,128)(2,1)}) custom-call(bf16[128,256]{1,0:T(8,128)(2,1)} %get-tuple-element.9.node_ref, bf16[128,4096]{1,0:T(8,128)(2,1)} %get-tuple-element.10.joint_ref, bf16[3,2,256,256]{3,2,1,0:T(8,128)(2,1)} %inner_q.1, bf16[3,256,256]{2,1,0:T(8,128)(2,1)} %inner_b.1, bf16[2,2,256,256]{3,2,1,0:T(8,128)(2,1)} %outer_q.1, ...), custom_call_target="tpu_custom_call" | custom-call | tf_op jit(solution)/shard_map/tree/pallas_call | solution.py:291
  35.3 18.0 %near.1.near_ref = f32[64,4096]{1,0:T(8,128)} custom-call(s32[4,3]{1,0:T(4,128)} %near_ref.1, bf16[128,4096]{1,0:T(8,128)(2,1)} %get-tuple-element.10.joint_ref, bf16[2,128,1024]{2,1,0:T(8,128)(2,1)} %get-tuple-element.12.halo_ref), custom_call_target="tpu_custom_call" | custom-call | tf_op jit(solution)/shard_map/near/pallas_call | solution.py:310
  53.4 0.0 copy-start
  53.4 0.0 copy-start.1
  53.4 12.5 %total.1 = (f32[64,4096]{1,0:T(8,128)}, f32[8,64]{1,0:T(8,128)}) custom-call(f32[64,256]{1,0:T(8,128)} %get-tuple-element.11.incoming_ref, bf16[4,256,256]{2,1,0:T(8,128)(2,1)} %trans_ref.3, bf16[4,1024,256]{2,1,0:T(8,128)(2,1)} %bases_ref.3, f32[64,4096]{1,0:T(8,128)} %near.1.near_ref, f32[64,4096]{1,0:T(8,128)} %bitcast.30, f32[64,4096]{1,0:T(8,128)} %bitcast.31), custom_call_target="tpu_custom_call" | custom-call | tf_op jit(solution)/shard_map/total/pallas_call | solution.py:321
  65.9 0.8 %fusion.2 = (f32[64]{0:T(128)S(1)}, f32[64]{0:T(128)S(1)}) fusion(f32[8,64]{1,0:T(8,128)} %get-tuple-element.13), kind=kLoop, calls=%fused_computation.6 | loop fusion | flops 512 | bytes 1536 | tf_op jit(solution)/shard_map/div | solution.py:343
  66.7 0.0 copy-done
  66.7 0.0 copy-done.1
  66.8 0.0 copy-start.2
  66.8 2.9 %add_bitcast_fusion = (f32[4096,64]{0,1:T(8,128)}, f32[4096,64]{0,1:T(8,128)}) fusion(f32[64]{0:T(128)S(1)} %get-tuple-element.15, f32[64,4096]{1,0:T(8,128)} %get-tuple-element.14, f32[64]{0:T(128)S(1)} %get-tuple-element.16, f32[4096,64]{0,1:T(8,128)S(1)} %copy-done.1, f32[4096,64]{0,1:T(8,128)S(1)} %copy-done), kind=kLoop, calls=%fused_computation | loop fusion | flops 1048576 | bytes 5243392 | tf_op jit(solution)/shard_map/transpose | solution.py:348
  69.6 0.0 copy-done.2
  69.6 1.2 %multiply_add_fusion = f32[4096,64]{0,1:T(8,128)} fusion(f32[4096,64]{0,1:T(8,128)S(1)} %copy-done.2, f32[4096,64]{0,1:T(8,128)S(1)} %copy-done, f32[64]{0:T(128)S(1)} %get-tuple-element.16), kind=kLoop, calls=%fused_computation.2 | loop fusion | flops 524288 | bytes 3145984 | tf_op jit(solution)/shard_map/add | solution.py:346
Async XLA Ops:
  53.4 13.4 %copy-start = (f32[4096,64]{0,1:T(8,128)S(1)}, f32[4096,64]{0,1:T(8,128)}, u32[]{:S(2)}) copy-start(f32[4096,64]{0,1:T(8,128)} %param.14) | copy-start | bytes 3145732
  53.4 13.4 %copy-start.1 = (f32[4096,64]{0,1:T(8,128)S(1)}, f32[4096,64]{0,1:T(8,128)}, u32[]{:S(2)}) copy-start(f32[4096,64]{0,1:T(8,128)} %param.13) | copy-start | bytes 3145732
  66.8 2.9 %copy-start.2 = (f32[4096,64]{0,1:T(8,128)S(1)}, f32[4096,64]{0,1:T(8,128)}, u32[]{:S(2)}) copy-start(f32[4096,64]{0,1:T(8,128)} %param.12) | copy-start | bytes 3145732

commit v2 on v1

v2 whole, which is shorter than its diff:
```python
import functools
import math

import jax
import jax.numpy as jnp
from jax import lax
from jax.experimental import pallas as pl
from jax.experimental.pallas import tpu as pltpu
from jax.sharding import PartitionSpec as P

MESH = pl.DeviceIdType.MESH
ridge = 2.0
f32 = jnp.float32
bf16 = jnp.bfloat16
vmem = pl.BlockSpec(memory_space=pltpu.VMEM)
smem = pl.BlockSpec(memory_space=pltpu.SMEM)


def nn(a, b):
    return jnp.dot(a, b, preferred_element_type=f32)


def nt(a, b):
    return lax.dot_general(a, b, (((1,), (1,)), ((), ())), preferred_element_type=f32)


def split(value):
    high = value.astype(bf16)
    low = (value - high.astype(f32)).astype(bf16)
    return jnp.concatenate([high, low], axis=0)


def fold(stacked):
    half = stacked.shape[0] // 2
    return stacked[:half] + stacked[half:]


def upward_kernel(points_ref, direction_ref, bases_ref, trans_ref, joint_ref, node_ref, acc):
    step = pl.program_id(0)
    dim = points_ref.shape[0]
    packed = direction_ref[...].astype(bf16)
    joint_ref[:dim, :] = points_ref[...]
    joint_ref[dim:, :] = packed
    term = fold(nn(split(nn(packed, bases_ref[0])), trans_ref[0]))

    @pl.when(step == 0)
    def _():
        acc[...] = term

    @pl.when(step > 0)
    def _():
        acc[...] += term

    @pl.when(step == pl.num_programs(0) - 1)
    def _():
        node_ref[...] = split(acc[...])


def step_kernel(
    groups, leaves, near_ref, node_ref, joint_ref, inner_q, inner_b, outer_q, outer_b,
    trans_hbm, bases_hbm, direction_hbm, residual_hbm, image_ref, sums_ref,
    sent, got, halo_ref, source, target, trans_ref, bases_ref, direction_ref, residual_ref, first, second,
    node_send, node_recv, halo_send, halo_recv, first_send, first_recv, second_send, second_recv, load_sem,
):
    loads = [
        pltpu.make_async_copy(src, dst, load_sem.at[n])
        for n, (src, dst) in enumerate(
            [(trans_hbm, trans_ref), (bases_hbm, bases_ref), (direction_hbm, direction_ref), (residual_hbm, residual_ref)]
        )
    ]
    for load in loads:
        load.start()
    grp = lax.axis_index("grp")
    pos = lax.axis_index("leaf")
    inner = inner_q.shape[0]
    outer = outer_q.shape[0]
    me = grp * leaves + pos
    count = groups * leaves
    right = lax.rem(me + 1, count)
    left = lax.rem(me + count - 1, count)
    right_id = (right // leaves, lax.rem(right, leaves))
    left_id = (left // leaves, lax.rem(left, leaves))
    levels = []
    for k in range(inner):
        bit = lax.rem(pos // (1 << k), 2)
        levels.append((bit, (grp, pos + (1 - 2 * bit) * (1 << k)), inner_q, inner_b, k))
    for k in range(outer):
        bit = lax.rem(grp // (1 << k), 2)
        levels.append((bit, (grp + (1 - 2 * bit) * (1 << k), pos), outer_q, outer_b, k))

    barrier = pltpu.get_barrier_semaphore()
    greeted = [left_id, right_id]
    greeted += [(grp, lax.rem(pos + o, leaves)) for o in range(1, leaves)]
    greeted += [(lax.rem(grp + o, groups), pos) for o in range(1, groups)]
    for who in greeted:
        pl.semaphore_signal(barrier, inc=1, device_id=who, device_id_type=MESH)

    leaf_dev, leaf = bases_ref.shape[:2]
    nrhs = image_ref.shape[0]
    dim = joint_ref.shape[0] - nrhs
    tile = min(leaf, 256)
    scale = 2.0 / dim * math.log2(math.e)

    def parts(pts):
        wide = pts.astype(f32)
        sq = jnp.sum(wide * wide, axis=0, keepdims=True)
        high = sq.astype(bf16).astype(f32)
        mid = (sq - high).astype(bf16).astype(f32)
        low = sq - high - mid
        row = lax.broadcasted_iota(jnp.int32, (128 - dim, pts.shape[1]), 0)

        def extra(first, second):
            ones = jnp.where(jnp.logical_and(row >= second, row < second + 3), 1.0, 0.0)
            return jnp.where(row == first, -high, jnp.where(row == first + 1, -mid, jnp.where(row == first + 2, -low, ones)))

        return wide, extra

    def put_source(slot, wide, extra):
        source[slot] = jnp.concatenate([2.0 * wide, extra(0, 3)], axis=0).T.astype(bf16)

    for i in range(leaf_dev):
        wide, extra = parts(joint_ref[:dim, i * leaf : (i + 1) * leaf])
        put_source(i + 1, wide, extra)
        target[i] = jnp.concatenate([wide, extra(3, 0)], axis=0).astype(bf16)

    def block(i, slot, values):
        acc = jnp.zeros((nrhs, leaf), f32)
        for t in range(leaf // tile):
            power = nn(source[slot, t * tile : (t + 1) * tile, :], target[i])
            kern = jnp.exp2(power * scale).astype(bf16)
            acc += nn(values(t), kern)
        return acc

    def own(j):
        return lambda t: joint_ref[dim:, j * leaf + t * tile : j * leaf + (t + 1) * tile]

    def edge(side):
        return lambda t: halo_ref[side, dim:, t * tile : (t + 1) * tile]

    def flagged(i, column, slot, values):
        flag = jnp.where(near_ref[i, column] >= 0, 1.0, 0.0).astype(f32)
        image_ref[:, i * leaf : (i + 1) * leaf] += flag * block(i, slot, values)

    def itself(i):
        image_ref[:, i * leaf : (i + 1) * leaf] = block(i, i + 1, own(i))

    jobs = [functools.partial(itself, i) for i in range(leaf_dev)]
    for i in range(leaf_dev - 1):
        jobs.append(functools.partial(flagged, i, 2, i + 2, own(i + 1)))
        jobs.append(functools.partial(flagged, i + 1, 1, i + 1, own(i)))

    pl.semaphore_wait(barrier, len(greeted))

    last = joint_ref.shape[1] - leaf
    halos = [
        pltpu.make_async_remote_copy(
            src_ref=joint_ref.at[:, pl.ds(last, leaf)], dst_ref=halo_ref.at[0],
            send_sem=halo_send.at[0], recv_sem=halo_recv.at[0], device_id=right_id, device_id_type=MESH,
        ),
        pltpu.make_async_remote_copy(
            src_ref=joint_ref.at[:, pl.ds(0, leaf)], dst_ref=halo_ref.at[1],
            send_sem=halo_send.at[1], recv_sem=halo_recv.at[1], device_id=left_id, device_id_type=MESH,
        ),
    ]

    def coupled(n):
        bit, _, _, b_ref, k = levels[n]
        other = got[n]
        mat = b_ref[k]
        return fold(jnp.where(bit == 0, nt(other, mat), nn(other, mat)))

    records = []
    for n, (bit, partner, q_ref, b_ref, k) in enumerate(levels):
        holder = node_ref if n == 0 else sent.at[n]
        copy = pltpu.make_async_remote_copy(
            src_ref=holder, dst_ref=got.at[n], send_sem=node_send.at[n], recv_sem=node_recv.at[n],
            device_id=partner, device_id_type=MESH,
        )
        copy.start()
        if n == inner:
            for halo in halos:
                halo.start()
        if n > 0:
            records.append(coupled(n - 1))
        final = n == len(levels) - 1
        if not final:
            mine = nn(holder[...], q_ref[k, bit])
        for job in jobs[n * len(jobs) // len(levels) : (n + 1) * len(jobs) // len(levels)]:
            job()
        copy.wait()
        if not final:
            sent[n + 1] = split(fold(mine + nn(got[n], q_ref[k, 1 - bit])))
    incoming = coupled(len(levels) - 1)
    for n in reversed(range(len(levels) - 1)):
        bit, _, q_ref, _, k = levels[n]
        incoming = records[n] + fold(nt(split(incoming), q_ref[k, bit]))

    stacked = split(incoming)
    for load in loads:
        load.wait()
    for i in range(leaf_dev):
        cols = slice(i * leaf, (i + 1) * leaf)
        leaf_in = fold(nt(stacked, trans_ref[i])).astype(bf16)
        image_ref[:, cols] += ridge * direction_ref[:, cols] + nt(leaf_in, bases_ref[i])

    for side, (i, column, slot) in enumerate([(0, 1, 0), (leaf_dev - 1, 2, leaf_dev + 1)]):
        halos[side].wait()
        put_source(slot, *parts(halo_ref[side, :dim, :]))
        flagged(i, column, slot, edge(side))

    sums = [jnp.zeros((nrhs, 128), f32)] * 4

    def narrow(value):
        out = value[:, :128]
        for c in range(1, value.shape[1] // 128):
            out += value[:, c * 128 : (c + 1) * 128]
        return out

    for i in range(leaf_dev):
        cols = slice(i * leaf, (i + 1) * leaf)
        way = direction_ref[:, cols]
        rest = residual_ref[:, cols]
        image = image_ref[:, cols]
        terms = (rest * rest, way * image, rest * image, image * image)
        sums = [s + narrow(t) for s, t in zip(sums, terms)]
    rows = [jnp.sum(s.T, axis=0, keepdims=True) for s in sums]
    first[pos] = jnp.concatenate(rows + [jnp.zeros((4, nrhs), f32)], axis=0)

    def exchange(slots, mine, count, send, recv, where):
        def copy(o, slot):
            return pltpu.make_async_remote_copy(
                src_ref=slots.at[slot], dst_ref=slots.at[slot], send_sem=send.at[o], recv_sem=recv.at[slot],
                device_id=where(lax.rem(mine + o, count)), device_id_type=MESH,
            )

        for o in range(1, count):
            copy(o, mine).start()
        for o in range(1, count):
            copy(o, lax.rem(mine + o, count)).wait_recv()
        for o in range(1, count):
            copy(o, mine).wait_send()
        out = slots[0]
        for s in range(1, count):
            out += slots[s]
        return out

    second[grp] = exchange(first, pos, leaves, first_send, first_recv, lambda t: (grp, t))
    sums_ref[...] = exchange(second, grp, groups, second_send, second_recv, lambda t: (t, pos))


def update_kernel(sums_ref, x_ref, r_ref, d_ref, image_ref, new_x, new_r, new_d):
    rr, pq, rq, qq = [sums_ref[c : c + 1, :] for c in range(4)]
    alpha = rr / pq
    fresh = rr - 2.0 * alpha * rq + alpha * alpha * qq
    nrhs = x_ref.shape[0]
    square = (nrhs, nrhs)
    diagonal = lax.broadcasted_iota(jnp.int32, square, 0) == lax.broadcasted_iota(jnp.int32, square, 1)

    def column(row):
        return jnp.sum(jnp.where(diagonal, jnp.broadcast_to(row, square), 0.0), axis=1, keepdims=True)

    step, blend = column(alpha), column(fresh / rr)
    way = d_ref[...]
    new_x[...] = x_ref[...] + step * way
    rest = r_ref[...] - step * image_ref[...]
    new_r[...] = rest
    new_d[...] = rest + blend * way


def body(groups, leaves, points, solution, residual, direction, near, bases, leaf_transfer,
         inner_transfer, inner_coupling, outer_transfer, outer_coupling):
    leaf_dev = near.shape[0]
    leaf, rank = bases.shape[1:]
    count, dim = points.shape
    nrhs = direction.shape[1]
    rows = dim + nrhs
    levels = inner_transfer.shape[0] + outer_transfer.shape[0]
    p, x, r, d = points.T, solution.T, residual.T, direction.T
    joint, node = pl.pallas_call(
        upward_kernel,
        grid=(leaf_dev,),
        in_specs=[
            pl.BlockSpec((dim, leaf), lambda i: (0, i)),
            pl.BlockSpec((nrhs, leaf), lambda i: (0, i)),
            pl.BlockSpec((1, leaf, rank), lambda i: (i, 0, 0)),
            pl.BlockSpec((1, rank, rank), lambda i: (i, 0, 0)),
        ],
        out_specs=[
            pl.BlockSpec((rows, leaf), lambda i: (0, i)),
            pl.BlockSpec((2 * nrhs, rank), lambda i: (0, 0)),
        ],
        out_shape=[
            jax.ShapeDtypeStruct((rows, count), bf16),
            jax.ShapeDtypeStruct((2 * nrhs, rank), bf16),
        ],
        scratch_shapes=[pltpu.VMEM((nrhs, rank), f32)],
        name="upward",
    )(p, d, bases, leaf_transfer)
    anywhere = pl.BlockSpec(memory_space=pl.ANY)
    sems = pltpu.SemaphoreType.DMA
    image, sums = pl.pallas_call(
        functools.partial(step_kernel, groups, leaves),
        in_specs=[smem] + [vmem] * 6 + [anywhere] * 4,
        out_specs=[vmem] * 2,
        out_shape=[
            jax.ShapeDtypeStruct((nrhs, count), f32),
            jax.ShapeDtypeStruct((8, nrhs), f32),
        ],
        scratch_shapes=[
            pltpu.VMEM((levels, 2 * nrhs, rank), bf16),
            pltpu.VMEM((levels, 2 * nrhs, rank), bf16),
            pltpu.VMEM((2, rows, leaf), bf16),
            pltpu.VMEM((leaf_dev + 2, leaf, 128), bf16),
            pltpu.VMEM((leaf_dev, 128, leaf), bf16),
            pltpu.VMEM(leaf_transfer.shape, bf16),
            pltpu.VMEM(bases.shape, bf16),
            pltpu.VMEM((nrhs, count), f32),
            pltpu.VMEM((nrhs, count), f32),
            pltpu.VMEM((leaves, 8, nrhs), f32),
            pltpu.VMEM((groups, 8, nrhs), f32),
            sems((levels,)), sems((levels,)), sems((2,)), sems((2,)),
            sems((leaves,)), sems((leaves,)), sems((groups,)), sems((groups,)), sems((4,)),
        ],
        compiler_params=pltpu.CompilerParams(collective_id=0, has_side_effects=True),
        name="step",
    )(near, node, joint, inner_transfer, inner_coupling, outer_transfer, outer_coupling, leaf_transfer, bases, d, r)
    wide = pl.BlockSpec((nrhs, leaf), lambda i: (0, i))
    outs = pl.pallas_call(
        update_kernel,
        grid=(leaf_dev,),
        in_specs=[pl.BlockSpec((8, nrhs), lambda i: (0, 0))] + [wide] * 4,
        out_specs=[wide] * 3,
        out_shape=[jax.ShapeDtypeStruct((nrhs, count), f32)] * 3,
        name="update",
    )(sums, x, r, d, image)
    return tuple(out.T for out in outs)


def solution(mesh):
    both = ("grp", "leaf")
    flat = P(both, None)
    deep = P(both, None, None)
    return jax.shard_map(
        functools.partial(body, mesh.shape["grp"], mesh.shape["leaf"]),
        mesh=mesh,
        in_specs=(flat, flat, flat, flat, flat, deep, deep, P(), P(), P(), P()),
        out_specs=(flat, flat, flat),
        check_vma=False,
    )
```

time: 71.1 us -> 53 us (0.75)
  Pallas kernels: 65.2 us -> 52 us
  other arithmetic: 4.89 us -> 0 us
    pallas_call x3 -> x2, Pallas kernels: 60.6 us -> 47.3 us  [the longest x1 42.8 us: body(): pl.pallas_call(functools.partial(step_kernel, groups, leaves), in_specs=[...]
    transpose x1 -> x0, other arithmetic: 2.88 us -> none  [body(): return ((x + alpha[:, None] * d).T, new_residual.T, (new_residual + beta[...]
    add x1 -> x0, other arithmetic: 1.17 us -> none  [body(): x + alpha[:, None] * d]
    div x1 -> x0, other arithmetic: 0.84 us -> none  [body(): beta = fresh / rr]
where the time goes in v2:
time: 53 us; the launch traced here: 52.7 us
  Pallas kernels  52 us (98%)
  between operations  0.64 us (1%)
    pallas_call x1, Pallas kernels, body(): pl.pallas_call(functools.partial(step_kernel, groups, leaves), in_specs=[...  42.8 us
    pallas_call x1, Pallas kernels, body(): pl.pallas_call(upward_kernel, grid=(leaf_dev,), in_specs=[pl.BlockSpec((d...  4.7 us
    pallas_call x1, Pallas kernels, body(): pl.pallas_call(update_kernel, grid=(leaf_dev,), in_specs=[pl.BlockSpec((8...  4.53 us

profile of v2, /device:TPU:0, one launch (start us, length us, event | category | flops | bytes accessed | tf_op | source)
XLA Modules:
  0.0 52.7 jit_solution(406825455464582242)
XLA Ops:
  0.6 4.7 %upward.1 = (bf16[128,4096]{1,0:T(8,128)(2,1)}, bf16[128,256]{1,0:T(8,128)(2,1)}) custom-call(bf16[64,4096]{1,0:T(8,128)(2,1)} %bitcast.13, f32[64,4096]{1,0:T(8,128)} %bitcast.7, bf16[4,1024,256]{2,1,0:T(8,128)(2,1)} %bases_hbm.1, bf16[4,256,256]{2,1,0:T(8,128)(2,1)} %trans_hbm.1), custom_call_target="tpu_custom_call" | custom-call | tf_op jit(solution)/shard_map/upward/pallas_call | solution.py:279
  5.3 42.8 %step.1 = (f32[64,4096]{1,0:T(8,128)}, f32[8,64]{1,0:T(8,128)}) custom-call(s32[4,3]{1,0:T(4,128)} %near_ref.1, bf16[128,256]{1,0:T(8,128)(2,1)} %get-tuple-element.10.node_ref, bf16[128,4096]{1,0:T(8,128)(2,1)} %get-tuple-element.11.joint_ref, bf16[3,2,256,256]{3,2,1,0:T(8,128)(2,1)} %inner_q.1, bf16[3,256,256]{2,1,0:T(8,128)(2,1)} %inner_b.1, ...), custom_call_target="tpu_custom_call" | custom-call | tf_op jit(solution)/shard_map/step/pallas_call | solution.py:301
  48.1 4.5 %update.1 = (f32[64,4096]{1,0:T(8,128)}, f32[64,4096]{1,0:T(8,128)}, f32[64,4096]{1,0:T(8,128)}) custom-call(f32[8,64]{1,0:T(8,128)} %get-tuple-element.12.sums_ref, f32[64,4096]{1,0:T(8,128)} %bitcast.12, f32[64,4096]{1,0:T(8,128)} %bitcast.11, f32[64,4096]{1,0:T(8,128)} %bitcast.9, f32[64,4096]{1,0:T(8,128)} %get-tuple-element.13.image_ref), custom_call_target="tpu_custom_call" | custom-call | tf_op jit(solution)/shard_map/update/pallas_call | solution.py:328

commit v3 on v2

--- a/solution.py
+++ b/solution.py
@@ -35,39 +35,18 @@
     return stacked[:half] + stacked[half:]
 
 
-def upward_kernel(points_ref, direction_ref, bases_ref, trans_ref, joint_ref, node_ref, acc):
-    step = pl.program_id(0)
-    dim = points_ref.shape[0]
-    packed = direction_ref[...].astype(bf16)
-    joint_ref[:dim, :] = points_ref[...]
-    joint_ref[dim:, :] = packed
-    term = fold(nn(split(nn(packed, bases_ref[0])), trans_ref[0]))
-
-    @pl.when(step == 0)
-    def _():
-        acc[...] = term
-
-    @pl.when(step > 0)
-    def _():
-        acc[...] += term
-
-    @pl.when(step == pl.num_programs(0) - 1)
-    def _():
-        node_ref[...] = split(acc[...])
-
-
 def step_kernel(
-    groups, leaves, near_ref, node_ref, joint_ref, inner_q, inner_b, outer_q, outer_b,
-    trans_hbm, bases_hbm, direction_hbm, residual_hbm, image_ref, sums_ref,
-    sent, got, halo_ref, source, target, trans_ref, bases_ref, direction_ref, residual_ref, first, second,
+    groups, leaves, near_ref, inner_q, inner_b, outer_q, outer_b,
+    points_hbm, trans_hbm, bases_hbm, direction_hbm, residual_hbm, image_ref, sums_ref, joint_ref, sent, got, halo_ref, source, target, trans_ref, bases_ref, direction_ref, residual_ref, first, second,
     node_send, node_recv, halo_send, halo_recv, first_send, first_recv, second_send, second_recv, load_sem,
 ):
-    loads = [
-        pltpu.make_async_copy(src, dst, load_sem.at[n])
-        for n, (src, dst) in enumerate(
-            [(trans_hbm, trans_ref), (bases_hbm, bases_ref), (direction_hbm, direction_ref), (residual_hbm, residual_ref)]
-        )
-    ]
+    leaf_dev, leaf = bases_ref.shape[:2]
+    nrhs = image_ref.shape[0]
+    dim = joint_ref.shape[0] - nrhs
+    pairs = [(direction_hbm, direction_ref), (trans_hbm, trans_ref)]
+    pairs += [(bases_hbm.at[i], bases_ref.at[i]) for i in range(leaf_dev)]
+    pairs += [(points_hbm, joint_ref.at[pl.ds(0, dim), :]), (residual_hbm, residual_ref)]
+    loads = [pltpu.make_async_copy(src, dst, load_sem.at[n]) for n, (src, dst) in enumerate(pairs)]
     for load in loads:
         load.start()
     grp = lax.axis_index("grp")
@@ -95,9 +74,18 @@
     for who in greeted:
         pl.semaphore_signal(barrier, inc=1, device_id=who, device_id_type=MESH)
 
-    leaf_dev, leaf = bases_ref.shape[:2]
-    nrhs = image_ref.shape[0]
-    dim = joint_ref.shape[0] - nrhs
+    loads[0].wait()
+    joint_ref[dim:, :] = direction_ref[...].astype(bf16)
+    loads[1].wait()
+    node = None
+    for i in range(leaf_dev):
+        loads[2 + i].wait()
+        skel = nn(joint_ref[dim:, i * leaf : (i + 1) * leaf], bases_ref[i])
+        term = nn(split(skel), trans_ref[i])
+        node = term if node is None else node + term
+    sent[0] = split(fold(node))
+    loads[-2].wait()
+
     tile = min(leaf, 256)
     scale = 2.0 / dim * math.log2(math.e)
 
@@ -118,11 +106,6 @@
     def put_source(slot, wide, extra):
         source[slot] = jnp.concatenate([2.0 * wide, extra(0, 3)], axis=0).T.astype(bf16)
 
-    for i in range(leaf_dev):
-        wide, extra = parts(joint_ref[:dim, i * leaf : (i + 1) * leaf])
-        put_source(i + 1, wide, extra)
-        target[i] = jnp.concatenate([wide, extra(3, 0)], axis=0).astype(bf16)
-
     def block(i, slot, values):
         acc = jnp.zeros((nrhs, leaf), f32)
         for t in range(leaf // tile):
@@ -142,12 +125,27 @@
         image_ref[:, i * leaf : (i + 1) * leaf] += flag * block(i, slot, values)
 
     def itself(i):
+        wide, extra = parts(joint_ref[:dim, i * leaf : (i + 1) * leaf])
+        put_source(i + 1, wide, extra)
+        target[i] = jnp.concatenate([wide, extra(3, 0)], axis=0).astype(bf16)
         image_ref[:, i * leaf : (i + 1) * leaf] = block(i, i + 1, own(i))
 
+    def beside(i):
+        here = jnp.where(near_ref[i, 2] >= 0, 1.0, 0.0).astype(f32)
+        there = jnp.where(near_ref[i + 1, 1] >= 0, 1.0, 0.0).astype(f32)
+        mine = joint_ref[dim:, i * leaf : (i + 1) * leaf]
+        values = own(i + 1)
+        acc = jnp.zeros((nrhs, leaf), f32)
+        for t in range(leaf // tile):
+            power = nn(source[i + 2, t * tile : (t + 1) * tile, :], target[i])
+            kern = jnp.exp2(power * scale).astype(bf16)
+            acc += nn(values(t), kern)
+            cols = slice((i + 1) * leaf + t * tile, (i + 1) * leaf + (t + 1) * tile)
+            image_ref[:, cols] += there * nt(mine, kern)
+        image_ref[:, i * leaf : (i + 1) * leaf] += here * acc
+
     jobs = [functools.partial(itself, i) for i in range(leaf_dev)]
-    for i in range(leaf_dev - 1):
-        jobs.append(functools.partial(flagged, i, 2, i + 2, own(i + 1)))
-        jobs.append(functools.partial(flagged, i + 1, 1, i + 1, own(i)))
+    jobs += [functools.partial(beside, i) for i in range(leaf_dev - 1)]
 
     pl.semaphore_wait(barrier, len(greeted))
 
@@ -171,7 +169,7 @@
 
     records = []
     for n, (bit, partner, q_ref, b_ref, k) in enumerate(levels):
-        holder = node_ref if n == 0 else sent.at[n]
+        holder = sent.at[n]
         copy = pltpu.make_async_remote_copy(
             src_ref=holder, dst_ref=got.at[n], send_sem=node_send.at[n], recv_sem=node_recv.at[n],
             device_id=partner, device_id_type=MESH,
@@ -196,8 +194,7 @@
         incoming = records[n] + fold(nt(split(incoming), q_ref[k, bit]))
 
     stacked = split(incoming)
-    for load in loads:
-        load.wait()
+    loads[-1].wait()
     for i in range(leaf_dev):
         cols = slice(i * leaf, (i + 1) * leaf)
         leaf_in = fold(nt(stacked, trans_ref[i])).astype(bf16)
@@ -276,37 +273,18 @@
     rows = dim + nrhs
     levels = inner_transfer.shape[0] + outer_transfer.shape[0]
     p, x, r, d = points.T, solution.T, residual.T, direction.T
-    joint, node = pl.pallas_call(
-        upward_kernel,
-        grid=(leaf_dev,),
-        in_specs=[
-            pl.BlockSpec((dim, leaf), lambda i: (0, i)),
-            pl.BlockSpec((nrhs, leaf), lambda i: (0, i)),
-            pl.BlockSpec((1, leaf, rank), lambda i: (i, 0, 0)),
-            pl.BlockSpec((1, rank, rank), lambda i: (i, 0, 0)),
-        ],
-        out_specs=[
-            pl.BlockSpec((rows, leaf), lambda i: (0, i)),
-            pl.BlockSpec((2 * nrhs, rank), lambda i: (0, 0)),
-        ],
-        out_shape=[
-            jax.ShapeDtypeStruct((rows, count), bf16),
-            jax.ShapeDtypeStruct((2 * nrhs, rank), bf16),
-        ],
-        scratch_shapes=[pltpu.VMEM((nrhs, rank), f32)],
-        name="upward",
-    )(p, d, bases, leaf_transfer)
     anywhere = pl.BlockSpec(memory_space=pl.ANY)
     sems = pltpu.SemaphoreType.DMA
     image, sums = pl.pallas_call(
         functools.partial(step_kernel, groups, leaves),
-        in_specs=[smem] + [vmem] * 6 + [anywhere] * 4,
+        in_specs=[smem] + [vmem] * 4 + [anywhere] * 5,
         out_specs=[vmem] * 2,
         out_shape=[
             jax.ShapeDtypeStruct((nrhs, count), f32),
             jax.ShapeDtypeStruct((8, nrhs), f32),
         ],
         scratch_shapes=[
+            pltpu.VMEM((rows, count), bf16),
             pltpu.VMEM((levels, 2 * nrhs, rank), bf16),
             pltpu.VMEM((levels, 2 * nrhs, rank), bf16),
             pltpu.VMEM((2, rows, leaf), bf16),
@@ -319,11 +297,11 @@
             pltpu.VMEM((leaves, 8, nrhs), f32),
             pltpu.VMEM((groups, 8, nrhs), f32),
             sems((levels,)), sems((levels,)), sems((2,)), sems((2,)),
-            sems((leaves,)), sems((leaves,)), sems((groups,)), sems((groups,)), sems((4,)),
+            sems((leaves,)), sems((leaves,)), sems((groups,)), sems((groups,)), sems((leaf_dev + 4,)),
         ],
         compiler_params=pltpu.CompilerParams(collective_id=0, has_side_effects=True),
         name="step",
-    )(near, node, joint, inner_transfer, inner_coupling, outer_transfer, outer_coupling, leaf_transfer, bases, d, r)
+    )(near, inner_transfer, inner_coupling, outer_transfer, outer_coupling, p, leaf_transfer, bases, d, r)
     wide = pl.BlockSpec((nrhs, leaf), lambda i: (0, i))
     outs = pl.pallas_call(
         update_kernel,

time: 53 us -> 46.6 us (0.88)
  Pallas kernels: 52 us -> 45.7 us
    pallas_call x1 -> x0, Pallas kernels: 4.7 us -> none  [body(): pl.pallas_call(upward_kernel, grid=(leaf_dev,), in_specs=[pl.BlockSpec((d...]
    pallas_call x1, Pallas kernels: 42.8 us -> 41.2 us  [body(): pl.pallas_call(functools.partial(step_kernel, groups, leaves), in_specs=[...]
where the time goes in v3:
time: 46.6 us; the launch traced here: 46.3 us
  Pallas kernels  45.7 us (98%)
  between operations  0.64 us (1%)
    pallas_call x1, Pallas kernels, body(): pl.pallas_call(functools.partial(step_kernel, groups, leaves), in_specs=[...  41.2 us
    pallas_call x1, Pallas kernels, body(): pl.pallas_call(update_kernel, grid=(leaf_dev,), in_specs=[pl.BlockSpec((8...  4.54 us

profile of v3, /device:TPU:0, one launch (start us, length us, event | category | flops | bytes accessed | tf_op | source)
XLA Modules:
  0.0 46.3 jit_solution(1212703108057913776)
XLA Ops:
  0.6 41.2 %step.1 = (f32[64,4096]{1,0:T(8,128)}, f32[8,64]{1,0:T(8,128)}) custom-call(s32[4,3]{1,0:T(4,128)} %near_ref.1, bf16[3,2,256,256]{3,2,1,0:T(8,128)(2,1)} %inner_q.1, bf16[3,256,256]{2,1,0:T(8,128)(2,1)} %inner_b.1, bf16[2,2,256,256]{3,2,1,0:T(8,128)(2,1)} %outer_q.1, bf16[2,256,256]{2,1,0:T(8,128)(2,1)} %outer_b.1, bf16[64,4096]{1,0:T(8,128)(2,1)} %bitcast.12, ...), custom_call_target="tpu_custom_call" | custom-call | tf_op jit(solution)/shard_map/step/pallas_call | solution.py:278
  41.8 4.5 %update.1 = (f32[64,4096]{1,0:T(8,128)}, f32[64,4096]{1,0:T(8,128)}, f32[64,4096]{1,0:T(8,128)}) custom-call(f32[8,64]{1,0:T(8,128)} %get-tuple-element.8.sums_ref, f32[64,4096]{1,0:T(8,128)} %bitcast.11, f32[64,4096]{1,0:T(8,128)} %bitcast.10, f32[64,4096]{1,0:T(8,128)} %bitcast.8, f32[64,4096]{1,0:T(8,128)} %get-tuple-element.9.image_ref), custom_call_target="tpu_custom_call" | custom-call | tf_op jit(solution)/shard_map/update/pallas_call | solution.py:306

commit v4 on v3

--- a/solution.py
+++ b/solution.py
@@ -36,8 +36,9 @@
 
 
 def step_kernel(
-    groups, leaves, near_ref, inner_q, inner_b, outer_q, outer_b,
-    points_hbm, trans_hbm, bases_hbm, direction_hbm, residual_hbm, image_ref, sums_ref, joint_ref, sent, got, halo_ref, source, target, trans_ref, bases_ref, direction_ref, residual_ref, first, second,
+    groups, leaves, near_ref, inner_q_hbm, inner_b_hbm, outer_q_hbm, outer_b_hbm,
+    points_hbm, trans_hbm, bases_hbm, direction_hbm, residual_hbm, image_ref, sums_ref,
+    inner_q, inner_b, outer_q, outer_b, joint_ref, sent, got, halo_ref, source, target, trans_ref, bases_ref, direction_ref, residual_ref, first, second,
     node_send, node_recv, halo_send, halo_recv, first_send, first_recv, second_send, second_recv, load_sem,
 ):
     leaf_dev, leaf = bases_ref.shape[:2]
@@ -46,6 +47,8 @@
     pairs = [(direction_hbm, direction_ref), (trans_hbm, trans_ref)]
     pairs += [(bases_hbm.at[i], bases_ref.at[i]) for i in range(leaf_dev)]
     pairs += [(points_hbm, joint_ref.at[pl.ds(0, dim), :]), (residual_hbm, residual_ref)]
+    matrices = len(pairs)
+    pairs += [(inner_q_hbm, inner_q), (inner_b_hbm, inner_b), (outer_q_hbm, outer_q), (outer_b_hbm, outer_b)]
     loads = [pltpu.make_async_copy(src, dst, load_sem.at[n]) for n, (src, dst) in enumerate(pairs)]
     for load in loads:
         load.start()
@@ -84,7 +87,8 @@
         term = nn(split(skel), trans_ref[i])
         node = term if node is None else node + term
     sent[0] = split(fold(node))
-    loads[-2].wait()
+    for load in [loads[matrices - 2]] + loads[matrices:]:
+        load.wait()
 
     tile = min(leaf, 256)
     scale = 2.0 / dim * math.log2(math.e)
@@ -194,7 +198,7 @@
         incoming = records[n] + fold(nt(split(incoming), q_ref[k, bit]))
 
     stacked = split(incoming)
-    loads[-1].wait()
+    loads[matrices - 1].wait()
     for i in range(leaf_dev):
         cols = slice(i * leaf, (i + 1) * leaf)
         leaf_in = fold(nt(stacked, trans_ref[i])).astype(bf16)
@@ -277,13 +281,17 @@
     sems = pltpu.SemaphoreType.DMA
     image, sums = pl.pallas_call(
         functools.partial(step_kernel, groups, leaves),
-        in_specs=[smem] + [vmem] * 4 + [anywhere] * 5,
+        in_specs=[smem] + [anywhere] * 9,
         out_specs=[vmem] * 2,
         out_shape=[
             jax.ShapeDtypeStruct((nrhs, count), f32),
             jax.ShapeDtypeStruct((8, nrhs), f32),
         ],
         scratch_shapes=[
+            pltpu.VMEM(inner_transfer.shape, bf16),
+            pltpu.VMEM(inner_coupling.shape, bf16),
+            pltpu.VMEM(outer_transfer.shape, bf16),
+            pltpu.VMEM(outer_coupling.shape, bf16),
             pltpu.VMEM((rows, count), bf16),
             pltpu.VMEM((levels, 2 * nrhs, rank), bf16),
             pltpu.VMEM((levels, 2 * nrhs, rank), bf16),
@@ -297,7 +305,7 @@
             pltpu.VMEM((leaves, 8, nrhs), f32),
             pltpu.VMEM((groups, 8, nrhs), f32),
             sems((levels,)), sems((levels,)), sems((2,)), sems((2,)),
-            sems((leaves,)), sems((leaves,)), sems((groups,)), sems((groups,)), sems((leaf_dev + 4,)),
+            sems((leaves,)), sems((leaves,)), sems((groups,)), sems((groups,)), sems((leaf_dev + 8,)),
         ],
         compiler_params=pltpu.CompilerParams(collective_id=0, has_side_effects=True),
         name="step",

time: 46.6 us -> 46 us (0.987)
  Pallas kernels: 45.7 us -> 45.1 us
    pallas_call x1, Pallas kernels: 41.2 us -> 40.6 us  [body(): pl.pallas_call(functools.partial(step_kernel, groups, leaves), in_specs=[...]
where the time goes in v4:
time: 46 us; the launch traced here: 45.8 us
  Pallas kernels  45.1 us (98%)
  between operations  0.64 us (1%)
    pallas_call x1, Pallas kernels, body(): pl.pallas_call(functools.partial(step_kernel, groups, leaves), in_specs=[...  40.6 us
    pallas_call x1, Pallas kernels, body(): pl.pallas_call(update_kernel, grid=(leaf_dev,), in_specs=[pl.BlockSpec((8...  4.54 us

profile of v4, /device:TPU:0, one launch (start us, length us, event | category | flops | bytes accessed | tf_op | source)
XLA Modules:
  0.0 45.8 jit_solution(15087936715082293378)
XLA Ops:
  0.6 40.6 %step.1 = (f32[64,4096]{1,0:T(8,128)}, f32[8,64]{1,0:T(8,128)}) custom-call(s32[4,3]{1,0:T(4,128)} %near_ref.1, bf16[3,2,256,256]{3,2,1,0:T(8,128)(2,1)} %inner_q_hbm.1, bf16[3,256,256]{2,1,0:T(8,128)(2,1)} %inner_b_hbm.1, bf16[2,2,256,256]{3,2,1,0:T(8,128)(2,1)} %outer_q_hbm.1, bf16[2,256,256]{2,1,0:T(8,128)(2,1)} %outer_b_hbm.1, ...), custom_call_target="tpu_custom_call" | custom-call | tf_op jit(solution)/shard_map/step/pallas_call | solution.py:282
  41.2 4.5 %update.1 = (f32[64,4096]{1,0:T(8,128)}, f32[64,4096]{1,0:T(8,128)}, f32[64,4096]{1,0:T(8,128)}) custom-call(f32[8,64]{1,0:T(8,128)} %get-tuple-element.8.sums_ref, f32[64,4096]{1,0:T(8,128)} %bitcast.11, f32[64,4096]{1,0:T(8,128)} %bitcast.10, f32[64,4096]{1,0:T(8,128)} %bitcast.8, f32[64,4096]{1,0:T(8,128)} %get-tuple-element.9.image_ref), custom_call_target="tpu_custom_call" | custom-call | tf_op jit(solution)/shard_map/update/pallas_call | solution.py:314
